TPU v7x, 32 devices: a whole 2x2x4 slice. The times are simulated.
32 devices in a mesh: beam: 16 (over z, y, x), tp: 2 (over core).
Axes of the slice: x: 2, y: 2, z: 4, core: 2. Of those that a mesh axis runs over, the one named last changes fastest.
Arguments:
- head_input: bfloat16 [32, 8192], P('beam', 'tp'), may hold values from -6 to 6
- gate_input: bfloat16 [32, 8192], P('beam', 'tp'), may hold values from -6 to 6
- state_maps: bfloat16 [32, 2, 1024], P('beam'), may hold values from -6 to 6
- step_input: bfloat16 [32, 128], P('beam', 'tp'), may hold values from -4 to 4
- step_bias: float32 [128], P('tp'), may hold values from -4 to -1
- decay_log: float32 [128], P('tp'), may hold values from -1 to 2.5
- skip_gain: float32 [128], P('tp'), may hold values from 0.5 to 2
- norm_gain: float32 [8192], P('tp'), may hold values from 0.5 to 1.5
- recurrent_state: float32 [32, 128, 64, 256], P('beam', 'tp'), may hold values from -80 to 80
- queries: bfloat16 [32, 8192], P('beam', 'tp'), may hold values from -80 to 80
- fresh_cache: bfloat16 [32, 2, 1024], P('beam', None, 'tp'), may hold values from -6 to 6
- cache_pool: bfloat16 [320, 2, 64, 1024], P('beam', None, None, 'tp'), may hold values from -6 to 6
- page_table: int32 [32, 10], P('beam'), may hold values from 0 to 19, as said below
- context_length: int32 [32], replicated, may hold values from 64 to 640, as said below
- parents: int32 [32], replicated, may hold values from 0 to 31, as said below
Outputs:
- child_state: float32 [32, 128, 64, 256], P('beam', 'tp')
- mixer_out: bfloat16 [32, 8192], P('beam', 'tp')
- attention_out: bfloat16 [32, 8192], P('beam', 'tp')
Inputs may be any that keep to these rules, and one draw needn't show every extreme that they name: `parents`: the parent of a child in block i of 2 beams lies in block i - 1, i or i + 1. In every block but the first exactly one child has its parent in the block below; in every block but the last exactly one has it in the block above; the others have theirs in their own block. `page_table`: in every block of 2 beams the rows name each of the block's 20 pages exactly once. `context_length`: some block of 2 beams has all lengths 640.
All inputs are finite; a program needn't handle non-finite values.
Results may differ from a plain program's by a relative error of at most 0.0035.
Values may be sent and summed in bfloat16 or wider, within the bound.
No kernel may reach another device: no remote copies, remote signals or barrier semaphores. Data moves between devices by JAX's collectives and lax.ppermute only.
A program may use at most 128 MiB of HBM per device.

v0:
```python
import jax
import jax.numpy as jnp
from jax import lax
from jax.sharding import PartitionSpec as P

HEADS = 128
GROUPS = 4
ATT_DIM = 128


def from_behind(value, axis, steps):
    count = lax.axis_size(axis)
    leading, last = (max(0, -steps), min(count, count - steps))
    return lax.ppermute(value, axis, [(source, source + steps) for source in range(leading, last)])


def attend(query_rows, cache_rows, pages, lengths):
    count = query_rows.shape[0]
    kv_width = cache_rows.shape[2]
    kv_heads = kv_width // ATT_DIM
    query_group = query_rows.shape[1] // kv_width
    positions = pages.shape[1] * pages.shape[3]
    factor = ATT_DIM ** (-0.5)
    grouped = query_rows.reshape(count, kv_heads, query_group, ATT_DIM)
    key_rows = pages[:, :, 0].reshape(count, positions, kv_heads, ATT_DIM)
    value_rows = pages[:, :, 1].reshape(count, positions, kv_heads, ATT_DIM)
    fresh_key = cache_rows[:, 0].reshape(count, kv_heads, ATT_DIM)
    fresh_value = cache_rows[:, 1].reshape(count, kv_heads, ATT_DIM).astype(jnp.float32)
    scores = (
        jnp.einsum("bgqd,btgd->bgqt", grouped, key_rows, preferred_element_type=jnp.float32)
        * factor
    )
    own_score = (
        jnp.einsum("bgqd,bgd->bgq", grouped, fresh_key, preferred_element_type=jnp.float32) * factor
    )
    live_mask = (jnp.arange(positions)[None, :] < lengths[:, None])[:, None, None, :]
    masked = jnp.where(live_mask, scores, -1e30)
    highest = jnp.maximum(jnp.max(masked, axis=-1), own_score)
    weights = jnp.where(live_mask, jnp.exp(masked - highest[..., None]), 0.0).astype(jnp.bfloat16)
    own_weight = jnp.exp(own_score - highest).astype(jnp.bfloat16).astype(jnp.float32)
    denom = jnp.sum(weights.astype(jnp.float32), axis=-1) + own_weight
    numer = jnp.einsum("bgqt,btgd->bgqd", weights, value_rows, preferred_element_type=jnp.float32)
    numer = numer + own_weight[..., None] * fresh_value[:, :, None, :]
    return (numer / denom[..., None]).reshape(count, -1).astype(jnp.bfloat16)


def shards(
    head_input,
    gate_input,
    state_maps,
    step_input,
    step_bias,
    decay_log,
    skip_gain,
    norm_gain,
    recurrent_state,
    queries,
    fresh_cache,
    cache_pool,
    page_table,
    context_length,
    parents,
):
    local_beams = head_input.shape[0]
    local_heads = step_input.shape[1]
    head_dim = recurrent_state.shape[2]
    state_dim = recurrent_state.shape[3]
    total_beams = parents.shape[0]
    device = lax.axis_index("beam")
    column = lax.axis_index("tp")
    own_parents = lax.dynamic_slice_in_dim(parents, device * local_beams, local_beams)
    source = own_parents // local_beams
    relative = source - device
    local_index = jnp.clip(own_parents - source * local_beams, 0, local_beams - 1)
    own_lengths = jnp.take(context_length, own_parents)
    previous = jnp.take(recurrent_state, local_index, axis=0)
    page_rows = jnp.take(page_table, local_index, axis=0)
    parent_pages = jnp.take(cache_pool, page_rows, axis=0)
    for direction in (1, -1):
        start = jnp.clip((device + direction) * local_beams, 0, total_beams - local_beams)
        block = lax.dynamic_slice_in_dim(parents, start, local_beams)
        found = block // local_beams == device
        index_out = jnp.clip(
            jnp.sum(jnp.where(found, block - device * local_beams, 0)), 0, local_beams - 1
        )
        outgoing = lax.dynamic_index_in_dim(recurrent_state, index_out, 0, keepdims=False)
        arrived = from_behind(outgoing, "beam", direction)
        taking = relative == -direction
        previous = jnp.where(taking[:, None, None, None], arrived[None], previous)
        rows_out = lax.dynamic_index_in_dim(page_table, index_out, 0, keepdims=False)
        pages_out = jnp.take(cache_pool, rows_out, axis=0)
        pages_in = from_behind(pages_out, "beam", direction)
        parent_pages = jnp.where(taking[:, None, None, None, None], pages_in[None], parent_pages)
    per_group = HEADS // GROUPS
    head_ids = column * local_heads + jnp.arange(local_heads)
    member = (head_ids[:, None] % GROUPS == jnp.arange(GROUPS)[None, :]).astype(jnp.float32)
    maps_all = state_maps.astype(jnp.float32).reshape(local_beams, 2, GROUPS, state_dim)
    input_maps = jnp.sum(member[None, :, :, None] * maps_all[:, 0][:, None], axis=2)
    output_maps = jnp.sum(member[None, :, :, None] * maps_all[:, 1][:, None], axis=2)
    inputs_x = head_input.astype(jnp.float32).reshape(local_beams, local_heads, head_dim)
    gate_values = gate_input.astype(jnp.float32).reshape(local_beams, local_heads, head_dim)
    step_size = jax.nn.softplus(step_input.astype(jnp.float32) + step_bias)
    retain = jnp.exp(-step_size * jnp.exp(decay_log))
    child_state = (
        retain[:, :, None, None] * previous
        + (step_size[:, :, None] * inputs_x)[..., None] * input_maps[:, :, None, :]
    )
    mixed_all = (
        jnp.sum(child_state * output_maps[:, :, None, :], axis=-1)
        + skip_gain[None, :, None] * inputs_x
    )
    gated_out = mixed_all * jax.nn.silu(gate_values)
    head_power = jnp.sum(gated_out * gated_out, axis=-1)
    partial_power = jnp.sum(head_power[:, :, None] * member[None], axis=1)
    group_power = lax.psum(partial_power, "tp")
    power_heads = jnp.sum(group_power[:, None, :] * member[None], axis=-1)
    inverse = lax.rsqrt(power_heads / (per_group * head_dim) + 1e-05)
    mixer_out = (
        (gated_out * inverse[..., None]).reshape(local_beams, local_heads * head_dim) * norm_gain
    ).astype(jnp.bfloat16)
    attention_out = attend(queries, fresh_cache, parent_pages, own_lengths)
    return (child_state, mixer_out, attention_out)


def solution(mesh):
    return jax.shard_map(
        shards,
        mesh=mesh,
        in_specs=(
            P("beam", "tp"),
            P("beam", "tp"),
            P("beam", None, None),
            P("beam", "tp"),
            P("tp"),
            P("tp"),
            P("tp"),
            P("tp"),
            P("beam", "tp", None, None),
            P("beam", "tp"),
            P("beam", None, "tp"),
            P("beam", None, None, "tp"),
            P("beam", None),
            P(),
            P(),
        ),
        out_specs=(P("beam", "tp", None, None), P("beam", "tp"), P("beam", "tp")),
        check_vma=False,
    )
```

profile of v0, /device:TPU:5, one launch (start us, length us, event | category | flops | bytes accessed | tf_op | source)
XLA Modules:
  0.0 280.4 jit_solution(742319542811114717)
XLA Ops:
  0.6 0.0 copy-start
  0.7 1.6 fusion.43
  3.5 0.0 copy-start.4
  3.5 7.8 %dynamic-slice_bitcast_fusion.1 = (f32[64,64,256]{2,1,0:T(8,128)}, f32[64,64,256]{2,1,0:T(8,128)}) fusion(f32[2,64,64,256]{3,2,1,0:T(8,128)} %param.25, s32[]{:T(128)S(6)} %min.20, s32[]{:T(128)S(6)} %min.22), kind=kLoop, calls=%fused_computation.14 | loop fusion | bytes 16777224 | tf_op jit(solution)/shard_map/jit(dynamic_index_in_dim)/squeeze | solution.py:86
  11.4 3.1 %collective-permute-start.1 = (f32[64,64,256]{2,1,0:T(8,128)}, f32[64,64,256]{2,1,0:T(8,128)}, u32[]{:S(2)}, u32[]{:S(2)}) collective-permute-start(f32[64,64,256]{2,1,0:T(8,128)} %get-tuple-element.23), channel_id=1, source_target_pairs={{0,2},{2,4},{4,6},{6,8},{8,10},{10,12},{12,14},{14,16},{16,18},{18... | collective-permute-start | bytes 12582920 | tf_op jit(solution)/shard_map/ppermute | solution.py:14
  14.5 3.1 %collective-permute-start = (f32[64,64,256]{2,1,0:T(8,128)}, f32[64,64,256]{2,1,0:T(8,128)}, u32[]{:S(2)}, u32[]{:S(2)}) collective-permute-start(f32[64,64,256]{2,1,0:T(8,128)} %get-tuple-element.22), channel_id=1, source_target_pairs={{2,0},{4,2},{6,4},{8,6},{10,8},{12,10},{14,12},{16,14},{18,16},{20... | collective-permute-start | bytes 12582920 | tf_op jit(solution)/shard_map/ppermute | solution.py:14
  17.5 0.0 copy-done.4
  17.6 0.0 copy-done
  17.6 1.8 gather_fusion.5
  19.4 2.6 broadcast_select_fusion.1
  22.0 4.1 %collective-permute-start.2 = (bf16[10,2,64,512]{3,2,1,0:T(8,128)(2,1)}, bf16[10,2,64,512]{3,2,1,0:T(8,128)(2,1)}, u32[]{:S(2)}, u32[]{:S(2)}) collective-permute-start(bf16[10,2,64,512]{3,2,1,0:T(8,128)(2,1)} %broadcast_select_fusion.1), channel_id=1, source_target_pairs={{2,0},{4,2},{6,4},{8,6},{10,8},{12,10},{14,12},{16,14},{18,16},{20... | collective-permute-start | bytes 3932168 | tf_op jit(solution)/shard_map/ppermute | solution.py:14
  26.1 1.8 gather_fusion.6
  27.9 2.6 broadcast_select_fusion
  30.5 1.9 collective-permute-start.3
  32.4 0.0 copy-start.8
  32.4 0.0 copy-start.9
  32.4 0.0 copy-start.5
  32.4 0.0 copy-start.15
  32.5 8.5 %fusion.50 = (f32[2,64,64,128]{3,2,1,0:T(8,128)}, f32[2,64,64,128]{3,2,1,0:T(8,128)}) fusion(f32[2,64,64,256]{3,2,1,0:T(8,128)} %param.25), kind=kLoop, calls=%fused_computation.107 | loop fusion | bytes 16777216 | tf_op jit(solution)/shard_map/jit(_take)/gather | solution.py:76
  41.0 0.1 subtract_compare_fusion.1
  41.0 0.1 compare_and_fusion.3
  41.1 0.6 gather_fusion.1
  41.7 0.1 compare_select_fusion
  41.8 0.1 reshape.255
  41.9 0.1 reshape.213
  42.0 4.9 %gather_fusion.4 = f32[2,64,64,128]{3,2,1,0:T(8,128)} fusion(f32[2,64,64,128]{3,2,1,0:T(8,128)} %get-tuple-element.25, s32[1024]{0:T(1024)S(1)} %pad_clamp_fusion.4), kind=kCustom, calls=%fused_computation.6 | custom fusion | bytes 8388616 | tf_op jit(solution)/shard_map/jit(_take)/gather | solution.py:76
  47.0 5.0 %gather_fusion.3 = f32[2,64,64,128]{3,2,1,0:T(8,128)} fusion(f32[2,64,64,128]{3,2,1,0:T(8,128)} %get-tuple-element.24, s32[1024]{0:T(1024)S(1)} %pad_clamp_fusion.4), kind=kCustom, calls=%fused_computation.5 | custom fusion | bytes 8388616 | tf_op jit(solution)/shard_map/jit(_take)/gather | solution.py:76
  52.0 0.1 reshape.216
  52.1 0.1 mul.219
  52.1 0.1 mul.220
  52.2 0.0 copy-start.10
  52.2 0.0 copy-start.14
  52.2 2.4 gather_fusion.2
  54.6 0.6 gather_fusion
  55.2 0.1 multiply_reduce_fusion.1
  55.4 0.1 compare_and_fusion.2
  55.5 0.1 iota_compare_fusion
  55.5 0.0 copy-done.12
  55.6 0.0 copy-done.10
  55.6 0.0 copy-done.14
  55.6 0.1 fusion.32
  55.7 0.1 broadcast_multiply_fusion
  55.8 166.2 %collective-permute-done.2 = bf16[10,2,64,512]{3,2,1,0:T(8,128)(2,1)} collective-permute-done((bf16[10,2,64,512]{3,2,1,0:T(8,128)(2,1)}, bf16[10,2,64,512]{3,2,1,0:T(8,128)(2,1)}, u32[]{:S(2)}, u32[]{:S(2)}) %collective-permute-start.2) | collective-permute-done | bytes 1310752 | tf_op jit(solution)/shard_map/ppermute | solution.py:14
  222.0 30.0 %collective-permute-done.3 = bf16[10,2,64,512]{3,2,1,0:T(8,128)(2,1)} collective-permute-done((bf16[10,2,64,512]{3,2,1,0:T(8,128)(2,1)}, bf16[10,2,64,512]{3,2,1,0:T(8,128)(2,1)}, u32[]{:S(2)}, u32[]{:S(2)}) %collective-permute-start.3) | collective-permute-done | bytes 1310752 | tf_op jit(solution)/shard_map/ppermute | solution.py:14
  252.0 3.9 %fusion.5 = bf16[2,10,2,64,512]{4,3,1,0,2:T(8,128)(2,1)S(1)} fusion(bf16[2,10,2,64,512]{4,3,2,1,0:T(8,128)(2,1)} %bitcast.56, pred[2]{0:T(512)(128)(4,1)S(1)} %get-tuple-element.33, pred[2]{0:T(512)(128)(4,1)S(1)} %get-tuple-element.16, pred[2,10]{1,0:T(4,128)(4,1)S(1)} %compare_and_fusion.2, bf16[10,2,64,512]{3,2,1,0:T(8,128)(2,1)} %collective-permute-done.2, ...), kind=kLoop, calls=%fused_computation.17 | loop fusion | flops 3932160 | bytes 7864344 | tf_op jit(solution)/shard_map/jit(_where)/select_n | solution.py:93
  255.9 1.9 fusion.51
  257.8 2.8 reshape_squeeze.12
  260.6 1.2 reshape_squeeze.10
  261.8 1.9 fusion.52
  263.7 0.2 convert_reduce_fusion
  263.9 0.4 fusion.28
  264.3 0.6 copy.72
  264.9 0.0 collective-permute-done.1
  264.9 0.0 collective-permute-done
  265.0 0.0 copy-start.1
  265.0 10.5 %multiply_reduce_fusion = (f32[2,64,64]{2,1,0:T(8,128)S(1)}, f32[2,64,64,256]{3,2,1,0:T(8,128)}) fusion(f32[2,64,256]{2,1,0:T(8,128)S(1)} %get-tuple-element.4, f32[2,64,256]{2,1,0:T(8,128)S(1)} %get-tuple-element.5, f32[2,64,64]{2,1,0:T(8,128)S(1)} %broadcast_multiply_fusion, f32[2,64,64,128]{3,2,1,0:T(8,128)} %gather_fusion.4, ...), kind=kLoop, calls=%fused_computation.12 | loop fusion | flops 18866176 | bytes 25494022 | tf_op jit(solution)/shard_map/reduce_sum | solution.py:109
  275.4 0.2 multiply_reduce_fusion.3
  275.6 0.1 multiply_reduce_fusion.5
  275.7 0.1 reduce_sum.88
  275.8 3.7 %psum.7 = f32[2,4]{1,0:T(2,128)S(1)} all-reduce(f32[2,4]{1,0:T(2,128)S(1)} %multiply_reduce_fusion.5), channel_id=1, replica_groups=mesh['beam'=16,'tp'=2] {'tp'}, use_global_device_ids=true, to_apply=%region_7.8 | all-reduce | flops 8 | bytes 64 | tf_op jit(solution)/shard_map/psum | solution.py:115
  279.5 0.1 multiply_reduce_fusion.4
  279.6 0.1 mul.235
  279.6 0.1 mul.236
  279.8 0.7 multiply_convert_fusion
  (35 shorter events, 0.2 us)
Async XLA Ops:
  0.6 17.0 %copy-start = (bf16[20,2,64,512]{3,2,1,0:T(8,128)(2,1)S(1)}, bf16[20,2,64,512]{3,2,1,0:T(8,128)(2,1)}, u32[]{:S(2)}) copy-start(bf16[20,2,64,512]{3,2,1,0:T(8,128)(2,1)} %param.28) | copy-start | bytes 7864324
  3.5 14.0 %copy-start.4 = (s32[2,10]{1,0:T(2,128)S(1)}, s32[2,10]{1,0:T(2,128)}, u32[]{:S(2)}) copy-start(s32[2,10]{1,0:T(2,128)} %param.29) | copy-start | bytes 244
  11.4 253.6 %collective-permute-start.1 = (f32[64,64,256]{2,1,0:T(8,128)}, f32[64,64,256]{2,1,0:T(8,128)}, u32[]{:S(2)}, u32[]{:S(2)}) collective-permute-start(f32[64,64,256]{2,1,0:T(8,128)} %get-tuple-element.23), channel_id=1, source_target_pairs={{0,2},{2,4},{4,6},{6,8},{8,10},{10,12},{12,14},{14,16},{16,18},{18... | collective-permute-start | bytes 12582920 | tf_op jit(solution)/shard_map/ppermute | solution.py:14
  14.5 250.5 %collective-permute-start = (f32[64,64,256]{2,1,0:T(8,128)}, f32[64,64,256]{2,1,0:T(8,128)}, u32[]{:S(2)}, u32[]{:S(2)}) collective-permute-start(f32[64,64,256]{2,1,0:T(8,128)} %get-tuple-element.22), channel_id=1, source_target_pairs={{2,0},{4,2},{6,4},{8,6},{10,8},{12,10},{14,12},{16,14},{18,16},{20... | collective-permute-start | bytes 12582920 | tf_op jit(solution)/shard_map/ppermute | solution.py:14
  22.0 200.0 %collective-permute-start.2 = (bf16[10,2,64,512]{3,2,1,0:T(8,128)(2,1)}, bf16[10,2,64,512]{3,2,1,0:T(8,128)(2,1)}, u32[]{:S(2)}, u32[]{:S(2)}) collective-permute-start(bf16[10,2,64,512]{3,2,1,0:T(8,128)(2,1)} %broadcast_select_fusion.1), channel_id=1, source_target_pairs={{2,0},{4,2},{6,4},{8,6},{10,8},{12,10},{14,12},{16,14},{18,16},{20... | collective-permute-start | bytes 3932168 | tf_op jit(solution)/shard_map/ppermute | solution.py:14
  30.5 221.5 %collective-permute-start.3 = (bf16[10,2,64,512]{3,2,1,0:T(8,128)(2,1)}, bf16[10,2,64,512]{3,2,1,0:T(8,128)(2,1)}, u32[]{:S(2)}, u32[]{:S(2)}) collective-permute-start(bf16[10,2,64,512]{3,2,1,0:T(8,128)(2,1)} %broadcast_select_fusion), channel_id=1, source_target_pairs={{0,2},{2,4},{4,6},{6,8},{8,10},{10,12},{12,14},{14,16},{16,18},{18... | collective-permute-start | bytes 3932168 | tf_op jit(solution)/shard_map/ppermute | solution.py:14
  32.4 8.5 %copy-start.8 = (s32[32]{0:T(128)S(1)}, s32[32]{0:T(128)}, u32[]{:S(2)}) copy-start(s32[32]{0:T(128)} %param.31) | copy-start | bytes 388
  32.4 9.5 %copy-start.9 = (bf16[2,2,1024]{2,1,0:T(2,128)(2,1)S(1)}, bf16[2,2,1024]{2,1,0:T(2,128)(2,1)}, u32[]{:S(2)}) copy-start(bf16[2,2,1024]{2,1,0:T(2,128)(2,1)} %param.19) | copy-start | bytes 24580
  32.4 9.5 %copy-start.5 = (bf16[2,4096]{1,0:T(2,128)(2,1)S(1)}, bf16[2,4096]{1,0:T(2,128)(2,1)}, u32[]{:S(2)}) copy-start(bf16[2,4096]{1,0:T(2,128)(2,1)} %param.17) | copy-start | bytes 49156
  32.4 9.6 %copy-start.15 = (f32[64]{0:T(128)S(1)}, f32[64]{0:T(128)}, u32[]{:S(2)}) copy-start(f32[64]{0:T(128)} %param.22) | copy-start | bytes 772
  47.0 5.0 %copy-start.6 = (bf16[2,4096]{1,0:T(2,128)(2,1)S(1)}, bf16[2,4096]{1,0:T(2,128)(2,1)}, u32[]{:S(2)}) copy-start(bf16[2,4096]{1,0:T(2,128)(2,1)} %param.18) | copy-start | bytes 49156
  47.0 5.1 %copy-start.11 = (f32[64]{0:T(128)S(1)}, f32[64]{0:T(128)}, u32[]{:S(2)}) copy-start(f32[64]{0:T(128)} %param.23) | copy-start | bytes 772
  52.2 2.4 copy-start.2
  52.2 3.3 %copy-start.12 = (f32[64]{0:T(128)S(1)}, f32[64]{0:T(128)}, u32[]{:S(2)}) copy-start(f32[64]{0:T(128)} %param.21) | copy-start | bytes 772
  52.2 3.3 %copy-start.13 = (bf16[2,64]{1,0:T(2,128)(2,1)S(1)}, bf16[2,64]{1,0:T(2,128)(2,1)}, u32[]{:S(2)}) copy-start(bf16[2,64]{1,0:T(2,128)(2,1)} %param.20) | copy-start | bytes 772
  52.2 3.4 %copy-start.10 = (bf16[2,2,512]{2,1,0:T(2,128)(2,1)S(1)}, bf16[2,2,512]{2,1,0:T(2,128)(2,1)}, u32[]{:S(2)}) copy-start(bf16[2,2,512]{2,1,0:T(2,128)(2,1)} %param.27) | copy-start | bytes 12292
  52.2 3.4 %copy-start.14 = (bf16[2,4096]{1,0:T(2,128)(2,1)S(1)}, bf16[2,4096]{1,0:T(2,128)(2,1)}, u32[]{:S(2)}) copy-start(bf16[2,4096]{1,0:T(2,128)(2,1)} %param.26) | copy-start | bytes 49156
  257.8 2.8 copy-start.3
  265.0 14.8 %copy-start.7 = (f32[4096]{0:T(1024)S(1)}, f32[4096]{0:T(1024)}, u32[]{:S(2)}) copy-start(f32[4096]{0:T(1024)} %param.24) | copy-start | bytes 49156
  265.0 15.5 %copy-start.1 = (bf16[20,2,64,512]{3,2,1,0:T(8,128)(2,1)S(1)}, bf16[20,2,64,512]{3,2,1,0:T(8,128)(2,1)}, u32[]{:S(2)}) copy-start(bf16[20,2,64,512]{3,2,1,0:T(8,128)(2,1)} %param.28) | copy-start | bytes 7864324
where the time goes:
time: 281 us; the launch traced here: 280 us
  waiting for transfers between devices  196 us (70%)
  local copies, waits for them, and re-layouts  40.6 us (14%)
  other arithmetic  23.1 us (8%)
  starting transfers between devices  12.2 us (4%)
  blocking collectives  3.66 us (1%)
    ppermute x4, waiting for transfers between devices, from_behind(): lax.ppermute(value, axis, [(source, source + steps) for source in range(l...  196 us
    gather x3, local copies, waits for them, and re-layouts, shards(): previous = jnp.take(recurrent_state, local_index, axis=0)  18.4 us
    ppermute x4, starting transfers between devices, from_behind(): lax.ppermute(value, axis, [(source, source + steps) for source in range(l...  12.2 us
    reduce_sum x1, other arithmetic, shards(): jnp.sum(child_state * output_maps[:, :, None, :], axis=-1)  10.5 us
    squeeze x1, local copies, waits for them, and re-layouts, shards(): lax.dynamic_index_in_dim(recurrent_state, index_out, 0, keepdims=False)  7.81 us
  transfers between devices with their start and end apart: 4, of which 2 were waited for; matrix products, arithmetic and copies ran while one was open for 16% of the time, Pallas kernels for 0%

commit v1 on v0

v1 whole, which is shorter than its diff:
```python
import functools

import jax
import jax.numpy as jnp
from jax import lax
from jax.experimental import pallas as pl
from jax.experimental.pallas import tpu as pltpu
from jax.sharding import PartitionSpec as P


HEADS = 128
GROUPS = 4
ATT_DIM = 128
CHUNK_EIGHTHS = (2, 3, 2, 1)
VMEM_LIMIT = 24 * 2**20


def exchange(value, axis, far):
    pairs = [(one, one + 1) for one in range(far, lax.axis_size(axis) - 1, 2)]
    return lax.ppermute(value, axis, pairs + [(two, one) for one, two in pairs])


def near_way(device):
    return 1 - 2 * lax.rem(device, 2)


def origin(parents, device, child, local_beams):
    offset = parents[device * local_beams + child] - device * local_beams
    way = jnp.where(offset < 0, -1, jnp.where(offset >= local_beams, 1, 0)).astype(jnp.int32)
    return way, jnp.clip(offset - way * local_beams, 0, local_beams - 1)


def wanted_by(parents, device, way, local_beams, total_beams):
    start = jnp.clip((device + way) * local_beams, 0, total_beams - local_beams)
    index = jnp.int32(0)
    for j in range(local_beams):
        offset = parents[start + j] - device * local_beams
        index = jnp.where((offset >= 0) & (offset < local_beams), offset, index)
    return index


def full_spec(space):
    return pl.BlockSpec(memory_space=space)


SMEM, VMEM, ANY = pltpu.SMEM, pltpu.VMEM, pl.ANY


def narrow_kernel(first, block, parents, device, state, *rest):
    *asking, wide, sems = rest
    near_out, far_out = asking[-2:]
    asking = asking[:-2]
    local_beams = state.shape[0]
    total_beams = parents.shape[0]
    here = device[0]
    way = near_way(here)
    tiles = wide.shape[1] // block
    picks = [wanted_by(parents, here, w, local_beams, total_beams) for w in (way, -way)]

    def copy(side, t):
        return pltpu.make_async_copy(
            state.at[picks[side], pl.ds(first + t * block, block)],
            wide.at[side, pl.ds(t * block, block)],
            sems.at[side, t],
        )

    for t in range(tiles):
        for side in range(2):
            copy(side, t).start()
    if asking:
        ask(parents, here, way, *asking)
    for t in range(tiles):
        for side, out in enumerate((near_out, far_out)):
            copy(side, t).wait()
            rows = slice(t * block, (t + 1) * block)
            out[rows] = wide[side, rows].astype(jnp.bfloat16)


def ask(parents, here, way, queries, fresh, maps, own_ask, near_ask, far_ask, rows):
    local_beams = queries.shape[0]
    for c in range(local_beams):
        row = 0
        for source in (
            queries[c : c + 1],
            fresh[c, 0:1],
            fresh[c, 1:2],
            maps[c, 1:2],
        ):
            source = source.astype(jnp.float32)
            for k in range(source.shape[1] // ATT_DIM):
                rows[row : row + 1] = source[:, k * ATT_DIM : (k + 1) * ATT_DIM]
                row += 1
        asked = rows[...].astype(jnp.bfloat16)
        own_ask[c] = asked
        from_way, _ = origin(parents, here, c, local_beams)

        @pl.when(from_way == way)
        def _():
            near_ask[...] = asked

        @pl.when(from_way == -way)
        def _():
            far_ask[...] = asked


def narrow(state, parents, place, first, count, block, asking=()):
    local_beams, _, head_dim, state_dim = state.shape
    out = jax.ShapeDtypeStruct((count, head_dim, state_dim), jnp.bfloat16)
    out_shape = [out, out]
    scratch = [
        pltpu.VMEM((2, count, head_dim, state_dim), jnp.float32),
        pltpu.SemaphoreType.DMA((2, count // block)),
    ]
    if asking:
        queries, fresh, maps = asking
        depth = (queries.shape[1] + 2 * fresh.shape[2] + maps.shape[2]) // ATT_DIM
        message = jax.ShapeDtypeStruct((depth, ATT_DIM), jnp.bfloat16)
        own = jax.ShapeDtypeStruct((local_beams, depth, ATT_DIM), jnp.bfloat16)
        out_shape += [own, message, message]
        scratch.append(pltpu.VMEM((depth, ATT_DIM), jnp.float32))

    def kernel(parents, place, state, *rest):
        if not asking:
            return narrow_kernel(first, block, parents, place, state, *rest)
        queries, fresh, maps, near, far, own, near_ask, far_ask, wide, sems, rows = rest
        return narrow_kernel(
            first, block, parents, place, state,
            queries, fresh, maps, own, near_ask, far_ask, rows, near, far, wide, sems,
        )

    return pl.pallas_call(
        kernel,
        out_shape=tuple(out_shape),
        in_specs=[full_spec(SMEM), full_spec(SMEM), full_spec(ANY)]
        + [full_spec(VMEM)] * len(asking),
        out_specs=tuple(full_spec(VMEM) for _ in out_shape),
        scratch_shapes=scratch,
        cost_estimate=pl.CostEstimate(
            flops=0, bytes_accessed=8 * count * head_dim * state_dim, transcendentals=0
        ),
        compiler_params=pltpu.CompilerParams(vmem_limit_bytes=VMEM_LIMIT),
        name="narrow",
    )(parents, place, state, *asking)


def grow_kernel(first, block, parents, device, state, near, far, drive, retain, maps, *rest):
    out, wide, columns, in_sems, out_sems, drive_sems = rest[-6:]
    local_beams, count = wide.shape[:2]
    tiles = count // block
    base = first // block
    here = device[0]
    way = near_way(here)
    origins = [origin(parents, here, c, local_beams) for c in range(local_beams)]

    def load(c):
        _, local = origins[c]
        return pltpu.make_async_copy(
            state.at[local, pl.ds(first, count)], wide.at[c], in_sems.at[c]
        )

    def load_drive(c):
        return pltpu.make_async_copy(
            drive.at[c, pl.ds(base, tiles)], columns.at[c], drive_sems.at[c]
        )

    def store(c, t):
        return pltpu.make_async_copy(
            wide.at[c, pl.ds(t * block, block)],
            out.at[c, pl.ds(first + t * block, block)],
            out_sems.at[c, t],
        )

    for c in range(local_beams):
        load_drive(c).start()

        @pl.when(origins[c][0] == 0)
        def _():
            load(c).start()

    for c in range(local_beams):
        from_way, _ = origins[c]
        load_drive(c).wait()

        @pl.when(from_way == 0)
        def _():
            load(c).wait()

        def tile(t, carry):
            def update(previous):
                for j in range(block):
                    head = t * block + j
                    wide[c, head] = (
                        retain[c, first + head] * previous(head)
                        + columns[c, t, :, j : j + 1] * maps[c, j % GROUPS : j % GROUPS + 1]
                    )

            @pl.when(from_way == 0)
            def _():
                update(lambda head: wide[c, head])

            @pl.when(from_way == way)
            def _():
                update(lambda head: near[head].astype(jnp.float32))

            @pl.when(from_way == -way)
            def _():
                update(lambda head: far[head].astype(jnp.float32))

            store(c, t).start()
            return carry

        lax.fori_loop(0, tiles, tile, 0)
    for c in range(local_beams):
        for t in range(tiles):
            store(c, t).wait()


def grow(parents, place, state, near, far, drive, retain, maps, first, block, partial):
    local_beams, _, head_dim, state_dim = state.shape
    count = near.shape[0]
    tiles = count // block
    spaces = [SMEM, SMEM, ANY, VMEM, VMEM, ANY, SMEM, VMEM]
    operands = [parents, place, state, near, far, drive, retain, maps]
    aliases = {}
    if partial is not None:
        aliases = {len(operands): 0}
        spaces.append(ANY)
        operands.append(partial)
    return pl.pallas_call(
        functools.partial(grow_kernel, first, block),
        out_shape=jax.ShapeDtypeStruct(state.shape, jnp.float32),
        in_specs=[full_spec(space) for space in spaces],
        out_specs=full_spec(ANY),
        scratch_shapes=[
            pltpu.VMEM((local_beams, count, head_dim, state_dim), jnp.float32),
            pltpu.VMEM((local_beams, tiles, head_dim, block), jnp.float32),
            pltpu.SemaphoreType.DMA((local_beams,)),
            pltpu.SemaphoreType.DMA((local_beams, tiles)),
            pltpu.SemaphoreType.DMA((local_beams,)),
        ],
        input_output_aliases=aliases,
        cost_estimate=pl.CostEstimate(
            flops=4 * local_beams * count * head_dim * state_dim,
            bytes_accessed=6 * local_beams * count * head_dim * state_dim,
            transcendentals=0,
        ),
        compiler_params=pltpu.CompilerParams(vmem_limit_bytes=VMEM_LIMIT),
        name="grow",
    )(*operands)


def attend_kernel(
    parents, device, table, lengths, own_ask, near_ask, far_ask, pool, out, maps_out, pages, sems
):
    local_beams, page_count = table.shape
    total_beams = parents.shape[0]
    kv_heads = pool.shape[3] // ATT_DIM
    query_heads = out.shape[1]
    group = query_heads // kv_heads
    positions = page_count * pool.shape[2]
    factor = ATT_DIM ** (-0.5)
    here = device[0]
    way = near_way(here)
    near_pick = wanted_by(parents, here, way, local_beams, total_beams)
    far_pick = wanted_by(parents, here, -way, local_beams, total_beams)
    served, copies = [], []
    for c in range(local_beams):
        from_way, local = origin(parents, here, c, local_beams)
        pick = jnp.where(from_way == 0, local, jnp.where(from_way == way, near_pick, far_pick))
        served.append((from_way, pick))
        copies.append(
            [
                pltpu.make_async_copy(pool.at[table[pick, j]], pages.at[c, j], sems.at[c, j])
                for j in range(page_count)
            ]
        )
    for some in copies:
        for copy in some:
            copy.start()
    for c in range(local_beams):
        from_way, pick = served[c]
        length = lengths[here * local_beams + pick]
        asked = jnp.where(
            from_way == 0,
            own_ask[c].astype(jnp.float32),
            jnp.where(
                from_way == way, near_ask[...].astype(jnp.float32), far_ask[...].astype(jnp.float32)
            ),
        )
        keys_at = query_heads
        values_at = query_heads + kv_heads
        maps_out[c] = asked[query_heads + 2 * kv_heads :]
        for copy in copies[c]:
            copy.wait()
        for g in range(kv_heads):
            lanes = slice(g * ATT_DIM, (g + 1) * ATT_DIM)
            rows = asked[g * group : (g + 1) * group]
            keys = pages[c, :, 0, :, lanes].reshape(positions, ATT_DIM)
            values = pages[c, :, 1, :, lanes].reshape(positions, ATT_DIM)
            own_key = asked[keys_at + g : keys_at + g + 1]
            own_value = asked[values_at + g : values_at + g + 1]
            scores = (
                lax.dot_general(
                    rows.astype(jnp.bfloat16),
                    keys,
                    (((1,), (1,)), ((), ())),
                    preferred_element_type=jnp.float32,
                )
                * factor
            )
            own_score = jnp.sum(rows * own_key, axis=1, keepdims=True) * factor
            live = lax.broadcasted_iota(jnp.int32, scores.shape, 1) < length
            masked = jnp.where(live, scores, -1e30)
            highest = jnp.maximum(jnp.max(masked, axis=1, keepdims=True), own_score)
            weights = jnp.where(live, jnp.exp(masked - highest), 0.0).astype(jnp.bfloat16)
            own_weight = jnp.exp(own_score - highest).astype(jnp.bfloat16).astype(jnp.float32)
            total = jnp.sum(weights.astype(jnp.float32), axis=1, keepdims=True) + own_weight
            summed = jnp.dot(weights, values, preferred_element_type=jnp.float32)
            out[c, g * group : (g + 1) * group] = (summed + own_weight * own_value) / total


def attend(parents, place, table, lengths, own_ask, near_ask, far_ask, pool, query_heads):
    local_beams, page_count = table.shape
    kv_heads = pool.shape[3] // ATT_DIM
    map_rows = own_ask.shape[1] - query_heads - 2 * kv_heads
    positions = page_count * pool.shape[2]
    return pl.pallas_call(
        attend_kernel,
        out_shape=(
            jax.ShapeDtypeStruct((local_beams, query_heads, ATT_DIM), jnp.float32),
            jax.ShapeDtypeStruct((local_beams, map_rows, ATT_DIM), jnp.float32),
        ),
        in_specs=[full_spec(SMEM)] * 4 + [full_spec(VMEM)] * 3 + [full_spec(ANY)],
        out_specs=(full_spec(VMEM), full_spec(VMEM)),
        scratch_shapes=[
            pltpu.VMEM((local_beams, page_count) + pool.shape[1:], jnp.bfloat16),
            pltpu.SemaphoreType.DMA((local_beams, page_count)),
        ],
        cost_estimate=pl.CostEstimate(
            flops=4 * local_beams * query_heads * positions * ATT_DIM,
            bytes_accessed=4 * local_beams * positions * pool.shape[3],
            transcendentals=local_beams * query_heads * positions,
        ),
        compiler_params=pltpu.CompilerParams(vmem_limit_bytes=VMEM_LIMIT),
        name="attend",
    )(parents, place, table, lengths, own_ask, near_ask, far_ask, pool)


def chunks_of(local_heads):
    unit = local_heads // 8
    if unit % GROUPS:
        return (local_heads // 2, local_heads // 2), GROUPS
    return tuple(eighths * unit for eighths in CHUNK_EIGHTHS), unit


def shards(
    head_input,
    gate_input,
    state_maps,
    step_input,
    step_bias,
    decay_log,
    skip_gain,
    norm_gain,
    recurrent_state,
    queries,
    fresh_cache,
    cache_pool,
    page_table,
    context_length,
    parents,
):
    local_beams, local_heads, head_dim, state_dim = recurrent_state.shape
    total_beams = parents.shape[0]
    query_width = queries.shape[1]
    device = lax.axis_index("beam").astype(jnp.int32)
    place = device.reshape(1)
    sizes, block = chunks_of(local_heads)
    firsts = [sum(sizes[:k]) for k in range(len(sizes))]

    arrived = []
    for k, (first, size) in enumerate(zip(firsts, sizes)):
        asking = () if k else (queries, fresh_cache, state_maps)
        near, far, *asked = narrow(recurrent_state, parents, place, first, size, block, asking)
        near = exchange(near, "beam", 0)
        far = exchange(far, "beam", 1)
        arrived.append((near, far))
        if asked:
            own_ask, near_ask, far_ask = asked
            near_ask = exchange(near_ask, "beam", 0)
            far_ask = exchange(far_ask, "beam", 1)

    attended, served_maps = attend(
        parents,
        place,
        page_table,
        context_length,
        own_ask,
        near_ask,
        far_ask,
        cache_pool,
        query_width // ATT_DIM,
    )
    way = near_way(device)
    origins = [origin(parents, device, c, local_beams) for c in range(local_beams)]
    near_pick = wanted_by(parents, device, way, local_beams, total_beams)
    far_pick = wanted_by(parents, device, -way, local_beams, total_beams)
    served_maps = served_maps.reshape(local_beams, 1, GROUPS, 1, state_dim)
    replies = []
    for c in range(local_beams):
        from_way, local = origins[c]
        pick = jnp.where(from_way == 0, local, jnp.where(from_way == way, near_pick, far_pick))
        parent_state = lax.dynamic_index_in_dim(recurrent_state, pick, 0, keepdims=False)
        parent_state = parent_state.reshape(-1, GROUPS, head_dim, state_dim)
        read_out = jnp.sum(parent_state * served_maps[c], axis=-1)
        replies.append(jnp.concatenate([attended[c].reshape(-1), read_out.reshape(-1)]))
    near_reply, far_reply = replies[0], replies[0]
    for c in range(1, local_beams):
        near_reply = jnp.where(origins[c][0] == way, replies[c], near_reply)
        far_reply = jnp.where(origins[c][0] == -way, replies[c], far_reply)
    near_reply = exchange(near_reply, "beam", 0)
    far_reply = exchange(far_reply, "beam", 1)
    answer = jnp.stack(
        [
            jnp.where(
                from_way == 0, replies[c], jnp.where(from_way == way, near_reply, far_reply)
            )
            for c, (from_way, _) in enumerate(origins)
        ]
    )
    attention_out = answer[:, :query_width].astype(jnp.bfloat16)

    inputs_x = head_input.astype(jnp.float32).reshape(local_beams, local_heads, head_dim)
    gate_values = gate_input.astype(jnp.float32).reshape(local_beams, local_heads, head_dim)
    step_size = jax.nn.softplus(step_input.astype(jnp.float32) + step_bias)
    retain = jnp.exp(-step_size * jnp.exp(decay_log))
    maps_all = state_maps.astype(jnp.float32).reshape(local_beams, 2, GROUPS, state_dim)
    drive = step_size[:, :, None] * inputs_x

    per_group = HEADS // GROUPS
    rows = local_heads // GROUPS
    overlap = jnp.sum(maps_all[:, 0] * maps_all[:, 1], axis=-1)
    overlap_heads = jnp.tile(overlap, (1, rows))
    read_back = answer[:, query_width:].reshape(local_beams, local_heads, head_dim)
    mixed_all = (
        retain[:, :, None] * read_back
        + drive * overlap_heads[:, :, None]
        + skip_gain[None, :, None] * inputs_x
    )
    gated_out = mixed_all * jax.nn.silu(gate_values)
    head_power = jnp.sum(gated_out * gated_out, axis=-1)
    partial_power = jnp.sum(head_power.reshape(local_beams, rows, GROUPS), axis=1)
    group_power = lax.psum(partial_power, "tp")
    inverse = lax.rsqrt(group_power / (per_group * head_dim) + 1e-05)
    inverse_heads = jnp.tile(inverse, (1, rows))
    mixer_out = (
        (gated_out * inverse_heads[..., None]).reshape(local_beams, local_heads * head_dim)
        * norm_gain
    ).astype(jnp.bfloat16)

    drive_columns = drive.reshape(local_beams, local_heads // block, block, head_dim).transpose(
        0, 1, 3, 2
    )
    child_state = None
    for first, (near, far) in zip(firsts, arrived):
        child_state = grow(
            parents,
            place,
            recurrent_state,
            near,
            far,
            drive_columns,
            retain,
            maps_all[:, 0],
            first,
            block,
            child_state,
        )
    return (child_state, mixer_out, attention_out)


def solution(mesh):
    return jax.shard_map(
        shards,
        mesh=mesh,
        in_specs=(
            P("beam", "tp"),
            P("beam", "tp"),
            P("beam", None, None),
            P("beam", "tp"),
            P("tp"),
            P("tp"),
            P("tp"),
            P("tp"),
            P("beam", "tp", None, None),
            P("beam", "tp"),
            P("beam", None, "tp"),
            P("beam", None, None, "tp"),
            P("beam", None),
            P(),
            P(),
        ),
        out_specs=(P("beam", "tp", None, None), P("beam", "tp"), P("beam", "tp")),
        check_vma=False,
    )
```

time: 281 us -> 115 us (0.41)
  the two profiles are of different devices: /device:TPU:5 before, /device:TPU:0 now
where the time goes in v1:
time: 115 us; the launch traced here: 114 us
  starting transfers between devices  25.5 us (22%)
  local copies, waits for them, and re-layouts  25.3 us (22%)
  waiting for transfers between devices  22.8 us (20%)
  Pallas kernels  22.7 us (20%)
  other arithmetic  10 us (9%)
  between operations  4.92 us (4%)
  blocking collectives  2.44 us (2%)
    ppermute x12, starting transfers between devices, exchange(): return lax.ppermute(value, axis, pairs + [(two, one) for one, two in pairs])  25.5 us
    ppermute x12, waiting for transfers between devices, exchange(): return lax.ppermute(value, axis, pairs + [(two, one) for one, two in pairs])  22.8 us
    unnamed x52, local copies, waits for them, and re-layouts  16 us
    pallas_call x4, Pallas kernels, grow(): pl.pallas_call(functools.partial(grow_kernel, first, block), out_shape=ja...  10.6 us
    pallas_call x1, Pallas kernels, attend(): pl.pallas_call(attend_kernel, out_shape=(jax.ShapeDtypeStruct((local_beam...  6.78 us
    pallas_call x4, Pallas kernels, narrow(): pl.pallas_call(kernel, out_shape=tuple(out_shape), in_specs=[full_spec(SM...  5.25 us
    reduce_sum x1, other arithmetic, shards(): read_out = jnp.sum(parent_state * served_maps[c], axis=-1)  4.66 us
    psum x1, blocking collectives, shards(): group_power = lax.psum(partial_power, 'tp')  2.44 us
  transfers between devices with their start and end apart: 12, of which 3 were waited for; matrix products, arithmetic and copies ran while one was open for 17% of the time, Pallas kernels for 17%

profile of v1, /device:TPU:0, one launch (start us, length us, event | category | flops | bytes accessed | tf_op | source)
XLA Modules:
  0.0 113.6 jit_solution(14303974729289976265)
XLA Ops:
  0.6 3.4 %copy-done = f32[2,64,64,256]{3,2,1,0:T(8,128)S(1)} copy-done((f32[2,64,64,256]{3,2,1,0:T(8,128)S(1)}, f32[2,64,64,256]{3,2,1,0:T(8,128)}, u32[]{:S(2)}) %copy-start) | copy-done | bytes 8388632
  4.0 0.7 copy-done.4
  4.7 0.7 copy-done.6
  5.4 0.7 copy-done.8
  6.1 0.7 copy-done.9
  6.8 1.9 %narrow.7 = (bf16[16,64,256]{2,1,0:T(8,128)(2,1)}, bf16[16,64,256]{2,1,0:T(8,128)(2,1)}, bf16[2,48,128]{2,1,0:T(8,128)(2,1)S(1)}, bf16[48,128]{1,0:T(8,128)(2,1)S(1)}, bf16[48,128]{1,0:T(8,128)(2,1)S(1)}) custom-call(s32[32]{0:T(128)S(1)} %copy-done.4, s32[1]{0:T(128)} %bitcast.place.device, f32[2,64,64,256]{3,2,1,0:T(8,128)S(1)} %copy-done, ...), custom_call_target="tpu_custom_call" | custom-call | bytes 2097152 | tf_op jit(solution)/shard_map/narrow/pallas_call | solution.py:131
  8.6 3.0 %collective-permute-start.8 = (bf16[48,128]{1,0:T(8,128)(2,1)S(1)}, bf16[48,128]{1,0:T(8,128)(2,1)S(1)}, u32[]{:S(2)}, u32[]{:S(2)}) collective-permute-start(bf16[48,128]{1,0:T(8,128)(2,1)S(1)} %get-tuple-element.25), channel_id=1, source_target_pairs={{0,2},{4,6},{8,10},{12,14},{16,18},{20,22},{24,26},{28,30},{2,0},{... | collective-permute-start | bytes 36872 | tf_op jit(solution)/shard_map/ppermute | solution.py:20
  11.7 0.7 collective-permute-start.9
  12.3 4.3 %collective-permute-start.6 = (bf16[16,64,256]{2,1,0:T(8,128)(2,1)}, bf16[16,64,256]{2,1,0:T(8,128)(2,1)}, u32[]{:S(2)}, u32[]{:S(2)}) collective-permute-start(bf16[16,64,256]{2,1,0:T(8,128)(2,1)} %get-tuple-element.22), channel_id=1, source_target_pairs={{0,2},{4,6},{8,10},{12,14},{16,18},{20,22},{24,26},{28,30},{2,0},{... | collective-permute-start | bytes 1572872 | tf_op jit(solution)/shard_map/ppermute | solution.py:20
  16.7 1.6 %collective-permute-start.7 = (bf16[16,64,256]{2,1,0:T(8,128)(2,1)}, bf16[16,64,256]{2,1,0:T(8,128)(2,1)}, u32[]{:S(2)}, u32[]{:S(2)}) collective-permute-start(bf16[16,64,256]{2,1,0:T(8,128)(2,1)} %get-tuple-element.23), channel_id=1, source_target_pairs={{2,4},{6,8},{10,12},{14,16},{18,20},{22,24},{26,28},{4,2},{8,6},{1... | collective-permute-start | bytes 1572872 | tf_op jit(solution)/shard_map/ppermute | solution.py:20
  18.3 1.8 %narrow.6 = (bf16[24,64,256]{2,1,0:T(8,128)(2,1)}, bf16[24,64,256]{2,1,0:T(8,128)(2,1)S(1)}) custom-call(s32[32]{0:T(128)S(1)} %copy-done.5, s32[1]{0:T(128)} %bitcast.place.device, f32[2,64,64,256]{3,2,1,0:T(8,128)S(1)} %copy-done), custom_call_target="tpu_custom_call" | custom-call | bytes 3145728 | tf_op jit(solution)/shard_map/narrow/pallas_call | solution.py:131
  20.1 0.9 copy-done.12
  21.1 3.6 %collective-permute-start.4 = (bf16[24,64,256]{2,1,0:T(8,128)(2,1)}, bf16[24,64,256]{2,1,0:T(8,128)(2,1)}, u32[]{:S(2)}, u32[]{:S(2)}) collective-permute-start(bf16[24,64,256]{2,1,0:T(8,128)(2,1)} %get-tuple-element.20), channel_id=1, source_target_pairs={{0,2},{4,6},{8,10},{12,14},{16,18},{20,22},{24,26},{28,30},{2,0},{... | collective-permute-start | bytes 2359304 | tf_op jit(solution)/shard_map/ppermute | solution.py:20
  24.7 0.1 mul.164
  24.8 0.1 reshape.81
  24.9 1.0 copy.22
  25.9 1.1 multiply_bitcast_fusion.drive
  27.1 0.7 fusion.8
  31.6 6.8 %attend.1 = (f32[2,32,128]{2,1,0:T(8,128)S(1)}, f32[2,8,128]{2,1,0:T(8,128)S(1)}) custom-call(s32[32]{0:T(128)S(1)} %copy-done.5, s32[1]{0:T(128)} %bitcast.place.device, s32[2,10]{1,0:T(2,128)S(1)} %copy-done.10, s32[32]{0:T(128)S(1)} %copy-done.11, bf16[2,48,128]{2,1,0:T(8,128)(2,1)S(1)} %get-tuple-element.24.own_ask, ...), custom_call_target="tpu_custom_call" | custom-call | flops 20971520 | bytes 2621440 | tf_op jit(solution)/shard_map/attend/pallas_call | solution.py:327
  38.5 4.7 %multiply_reduce_fusion.1 = (f32[64,64]{1,0:T(8,128)S(1)}, f32[64,64]{1,0:T(8,128)S(1)}) fusion(f32[2,64,64,256]{3,2,1,0:T(8,128)} %state.15, s32[]{:T(128)S(6)} %select_n.113, f32[64,256]{1,0:T(8,128)S(1)} %mul.178, f32[64,256]{1,0:T(8,128)S(1)} %mul.184, s32[]{:T(128)S(6)} %select_n.121), kind=kLoop, calls=%fused_computation.1 | loop fusion | flops 4186112 | bytes 8552456 | tf_op jit(solution)/shard_map/reduce_sum | solution.py:415
  43.2 0.1 reshape.84
  43.3 0.1 reshape.85
  43.4 0.7 collective-permute-start.11
  44.1 0.1 fusion.6
  44.2 0.7 reshape.87
  44.9 3.4 %copy-done.1 = f32[2,64,64,256]{3,2,1,0:T(8,128)S(1)} copy-done((f32[2,64,64,256]{3,2,1,0:T(8,128)S(1)}, f32[2,64,64,256]{3,2,1,0:T(8,128)}, u32[]{:S(2)}) %copy-start.1) | copy-done | bytes 8388632
  48.3 0.8 narrow.5
  49.2 0.8 copy-done.14
  50.0 0.7 narrow.4
  50.7 0.7 copy-done.15
  51.4 0.1 tile.17
  51.5 0.7 reshape.88
  52.2 0.1 mul.169
  52.3 0.7 mul.170
  53.0 0.1 mul.188
  53.1 0.7 mul.189
  53.8 0.1 mul.192
  53.8 0.7 mul.193
  54.6 2.9 %collective-permute-done.10 = f32[8192]{0:T(1024)S(1)} collective-permute-done((f32[8192]{0:T(1024)S(1)}, f32[8192]{0:T(1024)S(1)}, u32[]{:S(2)}, u32[]{:S(2)}) %collective-permute-start.10) | collective-permute-done | bytes 32800 | tf_op jit(solution)/shard_map/ppermute | solution.py:20
  57.5 0.7 collective-permute-start.5
  58.2 0.6 copy-done.21
  58.8 4.5 %collective-permute-start.2 = (bf16[16,64,256]{2,1,0:T(8,128)(2,1)}, bf16[16,64,256]{2,1,0:T(8,128)(2,1)S(1)}, u32[]{:S(2)}, u32[]{:S(2)}) collective-permute-start(bf16[16,64,256]{2,1,0:T(8,128)(2,1)} %copy-done.14), channel_id=1, source_target_pairs={{0,2},{4,6},{8,10},{12,14},{16,18},{20,22},{24,26},{28,30},{2,0},{... | collective-permute-start | bytes 1572872 | tf_op jit(solution)/shard_map/ppermute | solution.py:20
  63.3 0.8 select_select_fusion
  64.1 0.7 reshape.86
  64.9 1.1 multiply_reduce_fusion.2
  66.0 0.1 reshape.89
  66.1 0.1 mul.195
  66.1 0.7 mul.196
  66.8 2.4 %psum.7 = f32[2,4]{1,0:T(2,128)S(1)} all-reduce(f32[2,4]{1,0:T(2,128)S(1)} %reduce_sum.49), channel_id=1, replica_groups=mesh['beam'=16,'tp'=2] {'tp'}, use_global_device_ids=true, to_apply=%region_5.6 | all-reduce | flops 8 | bytes 64 | tf_op jit(solution)/shard_map/psum | solution.py:453
  69.3 0.1 tile.19
  69.4 0.7 mul.209
  70.1 0.9 mul.210
  71.1 0.7 collective-permute-start.3
  71.8 1.5 %multiply_convert_fusion = bf16[2,4096]{1,0:T(2,128)(2,1)} fusion(f32[2,4096]{1,0:T(2,128)S(1)} %mul.210, f32[2,4096]{1,0:T(2,128)} %mul.193, f32[2,4096]{1,0:T(2,128)} %mul.189, f32[2,4096]{1,0:T(2,128)} %mul.170, f32[4096]{0:T(1024)} %param.22, f32[4096]{0:T(1024)} %mul.196, bf16[2,4096]{1,0:T(2,128)(2,1)} %param.16, bf16[2,4096]{1,0:T(2,128)(2,1)S(1)} %copy-done.16, ...), kind=kLoop, calls=%fused_computation.13 | loop fusion | flops 139264 | bytes 278528 | tf_op jit(solution)/shard_map/convert_element_type | solution.py:459
  73.3 5.1 %collective-permute-start = (bf16[8,64,256]{2,1,0:T(8,128)(2,1)}, bf16[8,64,256]{2,1,0:T(8,128)(2,1)S(1)}, u32[]{:S(2)}, u32[]{:S(2)}) collective-permute-start(bf16[8,64,256]{2,1,0:T(8,128)(2,1)} %copy-done.15), channel_id=1, source_target_pairs={{0,2},{4,6},{8,10},{12,14},{16,18},{20,22},{24,26},{28,30},{2,0},{... | collective-permute-start | bytes 786440 | tf_op jit(solution)/shard_map/ppermute | solution.py:20
  78.4 0.7 collective-permute-start.1
  79.1 0.6 fusion.2
  79.7 3.4 %copy-done.2 = f32[2,64,64,256]{3,2,1,0:T(8,128)S(1)} copy-done((f32[2,64,64,256]{3,2,1,0:T(8,128)S(1)}, f32[2,64,64,256]{3,2,1,0:T(8,128)}, u32[]{:S(2)}) %copy-start.2) | copy-done | bytes 8388632
  83.1 3.0 %grow.4.rest_0_ = f32[2,64,64,256]{3,2,1,0:T(8,128)} custom-call(s32[32]{0:T(128)S(1)} %copy-done.5, s32[1]{0:T(128)} %bitcast.place.device, f32[2,64,64,256]{3,2,1,0:T(8,128)S(1)} %copy-done.2, bf16[16,64,256]{2,1,0:T(8,128)(2,1)} %collective-permute-done.6.near, bf16[16,64,256]{2,1,0:T(8,128)(2,1)} %collective-permute-done.7.far, ...), custom_call_target="tpu_custom_call" | custom-call | flops 2097152 | bytes 3145728 | tf_op jit(solution)/shard_map/grow/pallas_call | solution.py:229
  86.1 3.4 %grow.5.rest_0_ = f32[2,64,64,256]{3,2,1,0:T(8,128)} custom-call(s32[32]{0:T(128)S(1)} %copy-done.5, s32[1]{0:T(128)} %bitcast.place.device, f32[2,64,64,256]{3,2,1,0:T(8,128)S(1)} %copy-done.2, bf16[24,64,256]{2,1,0:T(8,128)(2,1)} %collective-permute-done.4.near, ...), custom_call_target="tpu_custom_call", output_to_operand_aliasing={{}: (8, {})} | custom-call | flops 3145728 | bytes 4718592 | tf_op jit(solution)/shard_map/grow/pallas_call | solution.py:229
  89.5 16.7 %collective-permute-done.2.near = bf16[16,64,256]{2,1,0:T(8,128)(2,1)S(1)} collective-permute-done((bf16[16,64,256]{2,1,0:T(8,128)(2,1)}, bf16[16,64,256]{2,1,0:T(8,128)(2,1)S(1)}, u32[]{:S(2)}, u32[]{:S(2)}) %collective-permute-start.2) | collective-permute-done | bytes 524320 | tf_op jit(solution)/shard_map/ppermute | solution.py:20
  106.3 2.3 %grow.6.rest_0_ = f32[2,64,64,256]{3,2,1,0:T(8,128)} custom-call(s32[32]{0:T(128)S(1)} %copy-done.5, s32[1]{0:T(128)} %bitcast.place.device, f32[2,64,64,256]{3,2,1,0:T(8,128)S(1)} %copy-done.2, bf16[16,64,256]{2,1,0:T(8,128)(2,1)S(1)} %collective-permute-done.2.near, ...), custom_call_target="tpu_custom_call", output_to_operand_aliasing={{}: (8, {})} | custom-call | flops 2097152 | bytes 3145728 | tf_op jit(solution)/shard_map/grow/pallas_call | solution.py:229
  108.6 3.2 %collective-permute-done.near = bf16[8,64,256]{2,1,0:T(8,128)(2,1)S(1)} collective-permute-done((bf16[8,64,256]{2,1,0:T(8,128)(2,1)}, bf16[8,64,256]{2,1,0:T(8,128)(2,1)S(1)}, u32[]{:S(2)}, u32[]{:S(2)}) %collective-permute-start) | collective-permute-done | bytes 262176 | tf_op jit(solution)/shard_map/ppermute | solution.py:20
  111.8 1.9 %grow.7 = f32[2,64,64,256]{3,2,1,0:T(8,128)} custom-call(s32[32]{0:T(128)S(1)} %copy-done.5, s32[1]{0:T(128)} %bitcast.place.device, f32[2,64,64,256]{3,2,1,0:T(8,128)S(1)} %copy-done.2, bf16[8,64,256]{2,1,0:T(8,128)(2,1)S(1)} %collective-permute-done.near, bf16[8,64,256]{2,1,0:T(8,128)(2,1)S(1)} %collective-permute-done.1.far, ...), custom_call_target="tpu_custom_call", output_to_operand_aliasing={{}: (8, {})} | custom-call | flops 1048576 | bytes 1572864 | tf_op jit(solution)/shard_map/grow/pallas_call | solution.py:229
  (69 shorter events, 0.4 us)
Async XLA Ops:
  0.6 3.4 %copy-start = (f32[2,64,64,256]{3,2,1,0:T(8,128)S(1)}, f32[2,64,64,256]{3,2,1,0:T(8,128)}, u32[]{:S(2)}) copy-start(f32[2,64,64,256]{3,2,1,0:T(8,128)} %state.15) | copy-start | bytes 25165828
  4.0 0.7 copy-start.4
  4.7 0.7 copy-start.6
  5.4 0.7 copy-start.8
  6.1 0.7 copy-start.9
  6.8 11.5 %copy-start.5 = (s32[32]{0:T(128)S(1)}, s32[32]{0:T(128)}, u32[]{:S(2)}) copy-start(s32[32]{0:T(128)} %parents.17) | copy-start | bytes 388
  8.6 22.9 %collective-permute-start.8 = (bf16[48,128]{1,0:T(8,128)(2,1)S(1)}, bf16[48,128]{1,0:T(8,128)(2,1)S(1)}, u32[]{:S(2)}, u32[]{:S(2)}) collective-permute-start(bf16[48,128]{1,0:T(8,128)(2,1)S(1)} %get-tuple-element.25), channel_id=1, source_target_pairs={{0,2},{4,6},{8,10},{12,14},{16,18},{20,22},{24,26},{28,30},{2,0},{... | collective-permute-start | bytes 36872 | tf_op jit(solution)/shard_map/ppermute | solution.py:20
  11.7 19.9 %collective-permute-start.9 = (bf16[48,128]{1,0:T(8,128)(2,1)S(1)}, bf16[48,128]{1,0:T(8,128)(2,1)S(1)}, u32[]{:S(2)}, u32[]{:S(2)}) collective-permute-start(bf16[48,128]{1,0:T(8,128)(2,1)S(1)} %get-tuple-element.26), channel_id=1, source_target_pairs={{2,4},{6,8},{10,12},{14,16},{18,20},{22,24},{26,28},{4,2},{8,6},{1... | collective-permute-start | bytes 36872 | tf_op jit(solution)/shard_map/ppermute | solution.py:20
  12.3 58.7 %collective-permute-start.6 = (bf16[16,64,256]{2,1,0:T(8,128)(2,1)}, bf16[16,64,256]{2,1,0:T(8,128)(2,1)}, u32[]{:S(2)}, u32[]{:S(2)}) collective-permute-start(bf16[16,64,256]{2,1,0:T(8,128)(2,1)} %get-tuple-element.22), channel_id=1, source_target_pairs={{0,2},{4,6},{8,10},{12,14},{16,18},{20,22},{24,26},{28,30},{2,0},{... | collective-permute-start | bytes 1572872 | tf_op jit(solution)/shard_map/ppermute | solution.py:20
  16.6 8.0 %copy-start.7 = (bf16[2,2,1024]{2,1,0:T(2,128)(2,1)S(1)}, bf16[2,2,1024]{2,1,0:T(2,128)(2,1)}, u32[]{:S(2)}) copy-start(bf16[2,2,1024]{2,1,0:T(2,128)(2,1)} %rest_2_.1) | copy-start | bytes 24580
  16.6 8.0 %copy-start.25 = (f32[64]{0:T(128)S(1)}, f32[64]{0:T(128)}, u32[]{:S(2)}) copy-start(f32[64]{0:T(128)} %param.20) | copy-start | bytes 772
  16.6 8.1 %copy-start.23 = (f32[64]{0:T(128)S(1)}, f32[64]{0:T(128)}, u32[]{:S(2)}) copy-start(f32[64]{0:T(128)} %param.19) | copy-start | bytes 772
  16.6 8.1 %copy-start.24 = (bf16[2,64]{1,0:T(2,128)(2,1)S(1)}, bf16[2,64]{1,0:T(2,128)(2,1)}, u32[]{:S(2)}) copy-start(bf16[2,64]{1,0:T(2,128)(2,1)} %param.18) | copy-start | bytes 772
  16.6 8.2 %copy-start.16 = (bf16[2,4096]{1,0:T(2,128)(2,1)S(1)}, bf16[2,4096]{1,0:T(2,128)(2,1)}, u32[]{:S(2)}) copy-start(bf16[2,4096]{1,0:T(2,128)(2,1)} %param.15) | copy-start | bytes 49156
  16.7 14.9 %copy-start.3 = (bf16[20,2,64,512]{3,2,1,0:T(8,128)(2,1)S(1)}, bf16[20,2,64,512]{3,2,1,0:T(8,128)(2,1)}, u32[]{:S(2)}) copy-start(bf16[20,2,64,512]{3,2,1,0:T(8,128)(2,1)} %pool.1) | copy-start | bytes 7864324
  16.7 14.9 %copy-start.10 = (s32[2,10]{1,0:T(2,128)S(1)}, s32[2,10]{1,0:T(2,128)}, u32[]{:S(2)}) copy-start(s32[2,10]{1,0:T(2,128)} %table.1) | copy-start | bytes 244
  16.7 14.9 %copy-start.11 = (s32[32]{0:T(128)S(1)}, s32[32]{0:T(128)}, u32[]{:S(2)}) copy-start(s32[32]{0:T(128)} %lengths.1) | copy-start | bytes 388
  16.7 56.6 %collective-permute-start.7 = (bf16[16,64,256]{2,1,0:T(8,128)(2,1)}, bf16[16,64,256]{2,1,0:T(8,128)(2,1)}, u32[]{:S(2)}, u32[]{:S(2)}) collective-permute-start(bf16[16,64,256]{2,1,0:T(8,128)(2,1)} %get-tuple-element.23), channel_id=1, source_target_pairs={{2,4},{6,8},{10,12},{14,16},{18,20},{22,24},{26,28},{4,2},{8,6},{1... | collective-permute-start | bytes 1572872 | tf_op jit(solution)/shard_map/ppermute | solution.py:20
  20.1 0.9 copy-start.12
  21.1 57.3 %collective-permute-start.4 = (bf16[24,64,256]{2,1,0:T(8,128)(2,1)}, bf16[24,64,256]{2,1,0:T(8,128)(2,1)}, u32[]{:S(2)}, u32[]{:S(2)}) collective-permute-start(bf16[24,64,256]{2,1,0:T(8,128)(2,1)} %get-tuple-element.20), channel_id=1, source_target_pairs={{0,2},{4,6},{8,10},{12,14},{16,18},{20,22},{24,26},{28,30},{2,0},{... | collective-permute-start | bytes 2359304 | tf_op jit(solution)/shard_map/ppermute | solution.py:20
  43.3 0.9 copy-start.17
  43.3 5.8 %copy-start.18 = (f32[4096]{0:T(1024)}, f32[4096]{0:T(1024)S(1)}, u32[]{:S(2)}) copy-start(f32[4096]{0:T(1024)S(1)} %get-tuple-element.38) | copy-start | bytes 49156
  43.4 14.1 %collective-permute-start.10 = (f32[8192]{0:T(1024)S(1)}, f32[8192]{0:T(1024)S(1)}, u32[]{:S(2)}, u32[]{:S(2)}) collective-permute-start(f32[8192]{0:T(1024)S(1)} %get-tuple-element.36), channel_id=1, source_target_pairs={{0,2},{4,6},{8,10},{12,14},{16,18},{20,22},{24,26},{28,30},{2,0},{... | collective-permute-start | bytes 98312 | tf_op jit(solution)/shard_map/ppermute | solution.py:20
  43.4 14.8 %collective-permute-start.11 = (f32[8192]{0:T(1024)S(1)}, f32[8192]{0:T(1024)S(1)}, u32[]{:S(2)}, u32[]{:S(2)}) collective-permute-start(f32[8192]{0:T(1024)S(1)} %get-tuple-element.35), channel_id=1, source_target_pairs={{2,4},{6,8},{10,12},{14,16},{18,20},{22,24},{26,28},{4,2},{8,6},{1... | collective-permute-start | bytes 98312 | tf_op jit(solution)/shard_map/ppermute | solution.py:20
  44.9 3.4 %copy-start.1 = (f32[2,64,64,256]{3,2,1,0:T(8,128)S(1)}, f32[2,64,64,256]{3,2,1,0:T(8,128)}, u32[]{:S(2)}) copy-start(f32[2,64,64,256]{3,2,1,0:T(8,128)} %state.15) | copy-start | bytes 25165828
  49.2 0.8 copy-start.14
  50.0 1.5 %copy-start.19 = (bf16[2,4096]{1,0:T(2,128)(2,1)S(1)}, bf16[2,4096]{1,0:T(2,128)(2,1)}, u32[]{:S(2)}) copy-start(bf16[2,4096]{1,0:T(2,128)(2,1)} %param.16) | copy-start | bytes 49156
  50.0 7.5 %copy-start.13 = (bf16[24,64,256]{2,1,0:T(8,128)(2,1)S(1)}, bf16[24,64,256]{2,1,0:T(8,128)(2,1)}, u32[]{:S(2)}) copy-start(bf16[24,64,256]{2,1,0:T(8,128)(2,1)} %copy-done.12) | copy-start | bytes 2359300
  50.0 14.9 %copy-start.22 = (f32[64]{0:T(128)S(1)}, f32[64]{0:T(128)}, u32[]{:S(2)}) copy-start(f32[64]{0:T(128)} %param.21) | copy-start | bytes 772
  50.7 0.7 copy-start.15
  57.5 0.7 copy-start.20
  57.5 28.6 %collective-permute-start.5 = (bf16[24,64,256]{2,1,0:T(8,128)(2,1)S(1)}, bf16[24,64,256]{2,1,0:T(8,128)(2,1)S(1)}, u32[]{:S(2)}, u32[]{:S(2)}) collective-permute-start(bf16[24,64,256]{2,1,0:T(8,128)(2,1)S(1)} %copy-done.13), channel_id=1, source_target_pairs={{2,4},{6,8},{10,12},{14,16},{18,20},{22,24},{26,28},{4,2},{8,6},{1... | collective-permute-start | bytes 2359304 | tf_op jit(solution)/shard_map/ppermute | solution.py:20
  58.2 0.6 copy-start.21
  58.8 47.4 %collective-permute-start.2 = (bf16[16,64,256]{2,1,0:T(8,128)(2,1)}, bf16[16,64,256]{2,1,0:T(8,128)(2,1)S(1)}, u32[]{:S(2)}, u32[]{:S(2)}) collective-permute-start(bf16[16,64,256]{2,1,0:T(8,128)(2,1)} %copy-done.14), channel_id=1, source_target_pairs={{0,2},{4,6},{8,10},{12,14},{16,18},{20,22},{24,26},{28,30},{2,0},{... | collective-permute-start | bytes 1572872 | tf_op jit(solution)/shard_map/ppermute | solution.py:20
  71.1 35.2 %collective-permute-start.3 = (bf16[16,64,256]{2,1,0:T(8,128)(2,1)S(1)}, bf16[16,64,256]{2,1,0:T(8,128)(2,1)S(1)}, u32[]{:S(2)}, u32[]{:S(2)}) collective-permute-start(bf16[16,64,256]{2,1,0:T(8,128)(2,1)S(1)} %get-tuple-element.19), channel_id=1, source_target_pairs={{2,4},{6,8},{10,12},{14,16},{18,20},{22,24},{26,28},{4,2},{8,6},{1... | collective-permute-start | bytes 1572872 | tf_op jit(solution)/shard_map/ppermute | solution.py:20
  73.3 38.5 %collective-permute-start = (bf16[8,64,256]{2,1,0:T(8,128)(2,1)}, bf16[8,64,256]{2,1,0:T(8,128)(2,1)S(1)}, u32[]{:S(2)}, u32[]{:S(2)}) collective-permute-start(bf16[8,64,256]{2,1,0:T(8,128)(2,1)} %copy-done.15), channel_id=1, source_target_pairs={{0,2},{4,6},{8,10},{12,14},{16,18},{20,22},{24,26},{28,30},{2,0},{... | collective-permute-start | bytes 786440 | tf_op jit(solution)/shard_map/ppermute | solution.py:20
  78.4 33.4 %collective-permute-start.1 = (bf16[8,64,256]{2,1,0:T(8,128)(2,1)S(1)}, bf16[8,64,256]{2,1,0:T(8,128)(2,1)S(1)}, u32[]{:S(2)}, u32[]{:S(2)}) collective-permute-start(bf16[8,64,256]{2,1,0:T(8,128)(2,1)S(1)} %get-tuple-element.17), channel_id=1, source_target_pairs={{2,4},{6,8},{10,12},{14,16},{18,20},{22,24},{26,28},{4,2},{8,6},{1... | collective-permute-start | bytes 786440 | tf_op jit(solution)/shard_map/ppermute | solution.py:20
  79.7 3.4 %copy-start.2 = (f32[2,64,64,256]{3,2,1,0:T(8,128)S(1)}, f32[2,64,64,256]{3,2,1,0:T(8,128)}, u32[]{:S(2)}) copy-start(f32[2,64,64,256]{3,2,1,0:T(8,128)} %state.15) | copy-start | bytes 25165828
